TPU v7x, 32 devices: a whole 2x2x4 slice. The times are simulated.
32 devices in a mesh: dp: 8 (over z, y), tensor: 4 (over x, core).
Axes of the slice: x: 2, y: 2, z: 4, core: 2. Of those that a mesh axis runs over, the one named last changes fastest.
Arguments:
- layer_in: bfloat16 [4096, 1024], P(('dp', 'tensor')), may hold values from -6 to 6
- doc_pos: int32 [4096], P('dp'), may hold values from 0 to 1999, as said below
- gain_attend: float32 [1024], replicated, may hold values from 0.5 to 1.5
- shift_attend: float32 [1024], replicated, may hold values from -3 to 3
- gain_dense: float32 [1024], replicated, may hold values from 0.5 to 1.5
- shift_dense: float32 [1024], replicated, may hold values from -3 to 3
- w_qkv: bfloat16 [1024, 3072], P('dp', 'tensor')
- b_qkv: float32 [3072], P('tensor'), may hold values from -3 to 3
- w_out: bfloat16 [1024, 1024], P('tensor', 'dp'), may hold values from -0.75 to 0.75
- b_out: float32 [1024], replicated, may hold values from -3 to 3
- w_up: bfloat16 [1024, 4096], P('dp', 'tensor'), may hold values from -0.1875 to 0.1875
- b_up: float32 [4096], P('tensor'), may hold values from -3 to 3
- w_down: bfloat16 [4096, 1024], P('tensor', 'dp'), may hold values from -0.09375 to 0.09375
- b_down: float32 [1024], replicated, may hold values from -3 to 3
- grad_out: bfloat16 [4096, 1024], P(('dp', 'tensor')), may hold values from -6 to 6
Outputs:
- layer_out: bfloat16 [4096, 1024], P(('dp', 'tensor'))
- grad_in: float32 [4096, 1024], P(('dp', 'tensor'))
- dgain_attend: float32 [1024], replicated
- dshift_attend: float32 [1024], replicated
- dgain_dense: float32 [1024], replicated
- dshift_dense: float32 [1024], replicated
- dw_qkv: float32 [1024, 3072], P('dp', 'tensor')
- db_qkv: float32 [3072], P('tensor')
- dw_out: float32 [1024, 1024], P('tensor', 'dp')
- db_out: float32 [1024], replicated
- dw_up: float32 [1024, 4096], P('dp', 'tensor')
- db_up: float32 [4096], P('tensor')
- dw_down: float32 [4096, 1024], P('tensor', 'dp')
- db_down: float32 [1024], replicated
Inputs may be any that keep to these rules, and one draw needn't show every extreme that they name: `doc_pos`: positions rise by one from token to token and restart at 0 where a document begins; the first token is at position 0; every whole document has 200 to 2000 tokens and one has exactly 2000; the last may be cut short, and a document may run across the border of two packed sequences.
All inputs are finite; a program needn't handle non-finite values.
Results may differ from a plain program's by a relative error of at most 0.02.
The roundings to bfloat16 on the way count: a program that leaves them out, or rounds other values in their place, can miss the bound.
Values may be sent and summed in bfloat16 or wider, within the bound.
No kernel may reach another device: no remote copies, remote signals or barrier semaphores. Data moves between devices by JAX's collectives and lax.ppermute only.
A program may use at most 128 MiB of HBM per device.

v0:
```python
import jax
import jax.numpy as jnp
from jax import lax
from jax.sharding import PartitionSpec as P

HEADS = 16
HD = 64
ROT = 16
SEQ = 4096
REACH = 4
EPS = 1e-05
MASKED = -1e30


def shifted_2(shard, axis, by):
    count = lax.axis_size(axis)
    pairs = [(i, i + by) for i in range(count) if 0 <= i + by < count]
    return lax.ppermute(shard, axis, pairs)


def normalize(x_float):
    average = jnp.mean(x_float, axis=-1, keepdims=True)
    centred = x_float - average
    inv_std = lax.rsqrt(jnp.mean(centred * centred, axis=-1, keepdims=True) + EPS)
    return (centred * inv_std, inv_std)


def norm_back(dnormed, normed, inv_std):
    return inv_std * (
        dnormed
        - jnp.mean(dnormed, axis=-1, keepdims=True)
        - normed * jnp.mean(dnormed * normed, axis=-1, keepdims=True)
    )


def rotary_tables(positions):
    half_rot = ROT // 2
    inv_freq = jnp.power(10000.0, -2.0 * jnp.arange(half_rot, dtype=jnp.float32) / ROT)
    angles = positions.astype(jnp.float32)[:, None] * inv_freq[None, :]
    cos_tab = jnp.cos(angles)
    sin_tab = jnp.sin(angles)
    return (
        jnp.concatenate([cos_tab, cos_tab], axis=-1),
        jnp.concatenate([sin_tab, sin_tab], axis=-1),
    )


def rotate(vectors, cos_tab, sin_tab):
    half_rot = ROT // 2
    leading = vectors[..., :ROT]
    turned = jnp.concatenate([-leading[..., half_rot:], leading[..., :half_rot]], axis=-1)
    return jnp.concatenate([leading * cos_tab + turned * sin_tab, vectors[..., ROT:]], axis=-1)


def rotate_back(upstream, cos_tab, sin_tab):
    half_rot = ROT // 2
    leading = upstream[..., :ROT]
    shifted = leading * sin_tab
    turned = jnp.concatenate([shifted[..., half_rot:], -shifted[..., :half_rot]], axis=-1)
    return jnp.concatenate([leading * cos_tab + turned, upstream[..., ROT:]], axis=-1)


def gelu_slope(preact):
    return (
        0.5 * (1.0 + lax.erf(preact * 0.7071067811865476))
        + preact * jnp.exp(-0.5 * preact * preact) * 0.3989422804014327
    )


def rows_product(left_rows, right_rows):
    return lax.dot_general(
        left_rows, right_rows, (((0,), (0,)), ((), ())), preferred_element_type=jnp.float32
    )


def shards(
    layer_in,
    doc_pos,
    gain_attend,
    shift_attend,
    gain_dense,
    shift_dense,
    w_qkv,
    b_qkv,
    w_out,
    b_out,
    w_up,
    b_up,
    w_down,
    b_down,
    grad_out,
):
    local_heads = HEADS // lax.axis_size("tensor")
    head_width = local_heads * HD
    score_scale = HD ** (-0.5)
    x_float = layer_in.astype(jnp.float32)
    normed, inv_std = normalize(x_float)
    first_in, second_in = (
        lax.all_gather(
            (normed * gain_attend + shift_attend).astype(jnp.bfloat16), "tensor", axis=0, tiled=True
        ),
        lax.all_gather(
            (normed * gain_dense + shift_dense).astype(jnp.bfloat16), "tensor", axis=0, tiled=True
        ),
    )
    row_count = first_in.shape[0]
    weights = (
        lax.all_gather(w_qkv, "dp", axis=0, tiled=True),
        lax.all_gather(w_out, "dp", axis=1, tiled=True),
        lax.all_gather(w_up, "dp", axis=0, tiled=True),
        lax.all_gather(w_down, "dp", axis=1, tiled=True),
    )
    full_qkv, full_out, full_up, full_down = weights
    joined_qkv = (jnp.dot(first_in, full_qkv, preferred_element_type=jnp.float32) + b_qkv).reshape(
        row_count, local_heads, 3, HD
    )
    cos_tab, sin_tab = rotary_tables(doc_pos)
    cos_tab = cos_tab[:, None, :]
    sin_tab = sin_tab[:, None, :]
    queries = rotate(joined_qkv[:, :, 0], cos_tab, sin_tab).astype(jnp.bfloat16)
    keys_rot = rotate(joined_qkv[:, :, 1], cos_tab, sin_tab).astype(jnp.bfloat16)
    values = joined_qkv[:, :, 2].astype(jnp.bfloat16)
    own_pair = jnp.stack(
        [keys_rot.reshape(row_count, head_width), values.reshape(row_count, head_width)], axis=0
    )
    key_pairs = [own_pair]
    for distance in range(1, REACH + 1):
        key_pairs.append(shifted_2(own_pair, "dp", distance))
    query_at = lax.axis_index("dp") * row_count + jnp.arange(row_count, dtype=jnp.int32)
    block_masks = []
    for distance in range(REACH + 1):
        key_at = query_at - distance * row_count
        offsets = query_at[:, None] - key_at[None, :]
        block_masks.append(
            (offsets >= 0)
            & (offsets <= doc_pos[:, None])
            & (query_at[:, None] // SEQ == key_at[None, :] // SEQ)
        )

    def block_scores(key_pair, allowed):
        keys_blk = key_pair[0].reshape(row_count, local_heads, HD)
        raw_scores = (
            jnp.einsum("qhd,khd->hqk", queries, keys_blk, preferred_element_type=jnp.float32)
            * score_scale
        )
        return jnp.where(allowed[None], raw_scores, MASKED)

    all_scores = [
        block_scores(key_pair, allowed) for key_pair, allowed in zip(key_pairs, block_masks)
    ]
    row_peak = all_scores[0].max(axis=-1)
    for scores in all_scores[1:]:
        row_peak = jnp.maximum(row_peak, scores.max(axis=-1))
    row_total = jnp.zeros_like(row_peak)
    for scores in all_scores:
        row_total = row_total + jnp.sum(jnp.exp(scores - row_peak[..., None]), axis=-1)
    logsum = row_peak + jnp.log(row_total)
    context = jnp.zeros((row_count, local_heads, HD), jnp.float32)
    for scores, key_pair in zip(all_scores, key_pairs):
        softmax = jnp.exp(scores - logsum[..., None]).astype(jnp.bfloat16)
        context = context + jnp.einsum(
            "hqk,khd->qhd",
            softmax,
            key_pair[1].reshape(row_count, local_heads, HD),
            preferred_element_type=jnp.float32,
        )
    context_b = context.reshape(row_count, head_width).astype(jnp.bfloat16)
    preact = jnp.dot(second_in, full_up, preferred_element_type=jnp.float32) + b_up
    hidden = jax.nn.gelu(preact, approximate=False).astype(jnp.bfloat16)
    branch = lax.psum_scatter(
        jnp.dot(context_b, full_out, preferred_element_type=jnp.float32)
        + jnp.dot(hidden, full_down, preferred_element_type=jnp.float32),
        "tensor",
        scatter_dimension=0,
        tiled=True,
    )
    layer_out = (x_float + b_out + b_down + branch).astype(jnp.bfloat16)
    grad_rows = lax.all_gather(grad_out, "tensor", axis=0, tiled=True)
    back_weights = (
        lax.all_gather(w_qkv, "dp", axis=0, tiled=True),
        lax.all_gather(w_out, "dp", axis=1, tiled=True),
        lax.all_gather(w_up, "dp", axis=0, tiled=True),
        lax.all_gather(w_down, "dp", axis=1, tiled=True),
    )
    back_qkv, back_out, back_up, back_down = back_weights
    dcontext = jnp.dot(grad_rows, back_out.T, preferred_element_type=jnp.float32).astype(
        jnp.bfloat16
    )
    dpreact = jnp.dot(grad_rows, back_down.T, preferred_element_type=jnp.float32) * gelu_slope(
        preact
    )
    dpreact_b = dpreact.astype(jnp.bfloat16)
    dw_out, dw_up, dw_down = (
        lax.psum_scatter(rows_product(context_b, grad_rows), "dp", scatter_dimension=1, tiled=True),
        lax.psum_scatter(rows_product(second_in, dpreact_b), "dp", scatter_dimension=0, tiled=True),
        lax.psum_scatter(rows_product(hidden, grad_rows), "dp", scatter_dimension=1, tiled=True),
    )
    dctx_heads = dcontext.reshape(row_count, local_heads, HD)
    deltas = jnp.sum(
        dctx_heads.astype(jnp.float32)
        * context_b.reshape(row_count, local_heads, HD).astype(jnp.float32),
        axis=-1,
    ).T
    dqueries = jnp.zeros((row_count, local_heads, HD), jnp.float32)
    pair_grads = []
    for key_pair, allowed in zip(key_pairs, block_masks):
        keys_blk = key_pair[0].reshape(row_count, local_heads, HD)
        values_blk = key_pair[1].reshape(row_count, local_heads, HD)
        scores = block_scores(key_pair, allowed)
        softmax_f = jnp.exp(scores - logsum[..., None])
        softmax_b = softmax_f.astype(jnp.bfloat16)
        dvalues = jnp.einsum(
            "hqk,qhd->khd", softmax_b, dctx_heads, preferred_element_type=jnp.float32
        )
        dsoftmax = jnp.einsum(
            "qhd,khd->hqk", dctx_heads, values_blk, preferred_element_type=jnp.float32
        )
        dscores = (softmax_f * (dsoftmax - deltas[..., None]) * score_scale).astype(jnp.bfloat16)
        dqueries = dqueries + jnp.einsum(
            "hqk,khd->qhd", dscores, keys_blk, preferred_element_type=jnp.float32
        )
        dkeys = jnp.einsum("hqk,qhd->khd", dscores, queries, preferred_element_type=jnp.float32)
        pair_grads.append(
            jnp.stack(
                [dkeys.reshape(row_count, head_width), dvalues.reshape(row_count, head_width)],
                axis=0,
            )
        )
    pair_total = pair_grads[0]
    for distance in range(1, REACH + 1):
        pair_total = pair_total + shifted_2(pair_grads[distance], "dp", -distance)
    dq_pre = rotate_back(dqueries, cos_tab, sin_tab)
    dk_pre = rotate_back(pair_total[0].reshape(row_count, local_heads, HD), cos_tab, sin_tab)
    dfused = jnp.stack(
        [dq_pre, dk_pre, pair_total[1].reshape(row_count, local_heads, HD)], axis=2
    ).reshape(row_count, 3 * head_width)
    bqkv_part = jnp.sum(dfused, axis=0)
    dfused_b = dfused.astype(jnp.bfloat16)
    dnorms = lax.psum_scatter(
        jnp.stack(
            [
                jnp.dot(dfused_b, back_qkv.T, preferred_element_type=jnp.float32),
                jnp.dot(dpreact_b, back_up.T, preferred_element_type=jnp.float32),
            ],
            axis=1,
        ),
        "tensor",
        scatter_dimension=0,
        tiled=True,
    )
    dfirst = dnorms[:, 0]
    dsecond = dnorms[:, 1]
    grad_float = grad_out.astype(jnp.float32)
    grad_in = grad_float + norm_back(dfirst * gain_attend + dsecond * gain_dense, normed, inv_std)
    dw_qkv = lax.psum_scatter(
        rows_product(first_in, dfused_b), "dp", scatter_dimension=0, tiled=True
    )
    db_qkv, db_up = lax.psum((bqkv_part, jnp.sum(dpreact, axis=0)), "dp")
    norm_sums = lax.psum(
        (
            jnp.sum(dfirst * normed, axis=0),
            jnp.sum(dfirst, axis=0),
            jnp.sum(dsecond * normed, axis=0),
            jnp.sum(dsecond, axis=0),
            jnp.sum(grad_float, axis=0),
        ),
        ("dp", "tensor"),
    )
    return (
        layer_out,
        grad_in,
        norm_sums[0],
        norm_sums[1],
        norm_sums[2],
        norm_sums[3],
        dw_qkv,
        db_qkv,
        dw_out,
        norm_sums[4],
        dw_up,
        db_up,
        dw_down,
        norm_sums[4],
    )


def solution(mesh):
    return jax.shard_map(
        shards,
        mesh=mesh,
        in_specs=(
            P(("dp", "tensor"), None),
            P("dp"),
            P(),
            P(),
            P(),
            P(),
            P("dp", "tensor"),
            P("tensor"),
            P("tensor", "dp"),
            P(),
            P("dp", "tensor"),
            P("tensor"),
            P("tensor", "dp"),
            P(),
            P(("dp", "tensor"), None),
        ),
        out_specs=(
            P(("dp", "tensor"), None),
            P(("dp", "tensor"), None),
            P(),
            P(),
            P(),
            P(),
            P("dp", "tensor"),
            P("tensor"),
            P("tensor", "dp"),
            P(),
            P("dp", "tensor"),
            P("tensor"),
            P("tensor", "dp"),
            P(),
        ),
        check_vma=False,
    )
```

profile of v0, /device:TPU:0, one launch (start us, length us, event | category | flops | bytes accessed | tf_op | source)
XLA Modules:
  0.0 799.1 jit_solution(18386472746760423022)
XLA Ops:
  8.0 1.1 convert_reduce_fusion
  9.1 1.2 fusion.63
  10.2 2.0 fusion.55
  15.0 29.6 %all_gather.27 = bf16[256,1024]{1,0:T(8,128)(2,1)S(1)} all-gather(bf16[256,128]{1,0:T(8,128)(2,1)S(1)} %copy-done.17), channel_id=1, replica_groups=mesh['dp'=8,'tensor'=4] {'dp'}, dimensions={1}, use_global_device_ids=true | all-gather | bytes 589824 | tf_op jit(solution)/shard_map/all_gather | solution.py:109
  44.7 2.7 fusion.39
  47.4 2.4 convolution_convert_fusion
  49.8 44.5 %all-gather.9.cloned.1.call-done = bf16[1024,768]{1,0:T(8,128)(2,1)} async-done(((bf16[128,768]{1,0:T(8,128)(2,1)}), bf16[1024,768]{1,0:T(8,128)(2,1)}) %all-gather.9.cloned.1.call-update) | async-done | bytes 1572880 | tf_op jit(solution)/shard_map/all_gather | solution.py:108
  94.3 2.7 convolution_add_fusion.1
  97.9 2.5 collective-permute-start
  100.4 3.4 collective-permute-start.1
  103.8 3.6 collective-permute-start.2
  107.4 1.3 collective-permute-start.3
  111.5 4.5 collective-permute-done.1
  117.0 15.4 %collective-permute-done.2 = bf16[2,512,256]{1,2,0:T(8,128)(2,1)S(1)} collective-permute-done((bf16[2,512,256]{1,2,0:T(8,128)(2,1)S(1)}, bf16[2,512,256]{1,2,0:T(8,128)(2,1)S(1)}, u32[]{:S(2)}, u32[]{:S(2)}) %collective-permute-start.2) | collective-permute-done | bytes 524320 | tf_op jit(solution)/shard_map/ppermute | solution.py:18
  133.4 10.9 %collective-permute-done.3 = bf16[2,512,256]{1,2,0:T(8,128)(2,1)S(1)} collective-permute-done((bf16[2,512,256]{1,2,0:T(8,128)(2,1)S(1)}, bf16[2,512,256]{1,2,0:T(8,128)(2,1)S(1)}, u32[]{:S(2)}, u32[]{:S(2)}) %collective-permute-start.3) | collective-permute-done | bytes 524320 | tf_op jit(solution)/shard_map/ppermute | solution.py:18
  145.3 5.1 exponential_reduce_fusion.3
  150.5 1.2 fusion.73
  151.7 1.3 fusion.108
  153.0 1.3 fusion.104
  154.2 1.3 convolution_add_fusion.5
  155.5 2.0 multiply_reduce_fusion
  157.5 1.6 multiply_convert_fusion.4
  159.2 1.6 multiply_convert_fusion.3
  160.8 1.6 multiply_convert_fusion.1
  162.4 1.6 multiply_convert_fusion
  164.1 1.8 multiply_convert_fusion.2
  165.9 1.2 fusion.96
  167.2 1.3 fusion.93
  168.4 1.3 fusion.106
  169.7 1.3 fusion.102
  171.7 1.1 pad_maximum_fusion.2
  172.8 1.3 collective-permute-start.4
  175.9 1.3 collective-permute-start.5
  177.9 1.1 pad_maximum_fusion.4
  179.0 1.3 collective-permute-start.6
  181.0 1.1 pad_maximum_fusion.5
  182.1 1.3 collective-permute-start.7
  187.1 1.2 fusion.99
  188.4 8.8 %fusion.12 = (bf16[512,1024]{1,0:T(8,128)(2,1)}, f32[512,1024]{1,0:T(8,128)}) fusion(f32[1024]{0:T(1024)S(1)} %copy-done.27, bf16[512,1024]{1,0:T(8,128)(2,1)} %all-gather.11.cloned.1.call-done, bf16[1024,1024]{1,0:T(8,128)(2,1)} %all-gather.13.cloned.1.call-done), kind=kOutput, calls=%fused_computation.35 | convolution fusion | flops 1108344832 | bytes 6295552 | tf_op jit(solution)/shard_map/dot_general | solution.py:168
  197.2 66.6 %all-gather.15.cloned.1.call-done = bf16[1024,1024]{1,0:T(8,128)(2,1)} async-done(((bf16[1024,128]{1,0:T(8,128)(2,1)}), bf16[1024,1024]{1,0:T(8,128)(2,1)}) %all-gather.15.cloned.1.call-update) | async-done | bytes 2097168 | tf_op jit(solution)/shard_map/all_gather | solution.py:111
  263.8 4.2 fusion.129
  268.0 1.3 convolution_bitcast_fusion
  269.3 21.3 %collective-permute-done.6 = f32[2,512,256]{1,2,0:T(8,128)} collective-permute-done((f32[2,512,256]{1,2,0:T(8,128)}, f32[2,512,256]{1,2,0:T(8,128)}, u32[]{:S(2)}, u32[]{:S(2)}) %collective-permute-start.6) | collective-permute-done | bytes 1048608 | tf_op jit(solution)/shard_map/ppermute | solution.py:18
  290.7 86.4 %collective-permute-done.7 = f32[2,512,256]{1,2,0:T(8,128)} collective-permute-done((f32[2,512,256]{1,2,0:T(8,128)}, f32[2,512,256]{1,2,0:T(8,128)}, u32[]{:S(2)}, u32[]{:S(2)}) %collective-permute-start.7) | collective-permute-done | bytes 1048608 | tf_op jit(solution)/shard_map/ppermute | solution.py:18
  377.1 2.8 fusion.35
  380.4 1.2 copy-done.25
  382.7 2.3 pad_maximum_fusion
  385.0 3.2 fusion.133
  388.3 1.8 convolution_add_fusion
  390.1 2.4 fusion.137
  392.6 4.0 fusion.136
  396.7 4.9 fusion.69
  401.9 4.5 fusion.138
  406.7 17.9 %all-reduce.1 = (f32[768]{0:T(1024)}, f32[1024]{0:T(1024)}) all-reduce(f32[768]{0:T(1024)S(1)} %reduce_sum.170, f32[1024]{0:T(1024)S(1)} %get-tuple-element.85), channel_id=1, replica_groups=mesh['dp'=8,'tensor'=4] {'dp'}, use_global_device_ids=true, to_apply=%region_27.28 | all-reduce | flops 1792 | bytes 14336 | tf_op jit(solution)/shard_map/psum | solution.py:258
  424.7 2.2 reduce-scatter.9.cloned.1.call-done
  426.9 1.3 slice_reduce_fusion
  428.2 1.5 fusion.120
  429.7 30.9 %reduce-scatter.7.cloned.1.call-done = f32[128,1024]{1,0:T(8,128)} async-done(((f32[512,1024]{1,0:T(8,128)}), f32[128,1024]{1,0:T(8,128)}) %reduce-scatter.7.cloned.1.call-update) | async-done | bytes 524304 | tf_op jit(solution)/shard_map/reduce_scatter | solution.py:170
  460.6 2.1 convert_reduce_fusion.1
  462.8 39.8 %all-reduce = (f32[1024]{0:T(1024)}, f32[1024]{0:T(1024)}, f32[1024]{0:T(1024)}, f32[1024]{0:T(1024)}, f32[1024]{0:T(1024)S(1)}) all-reduce(f32[1024]{0:T(1024)S(1)} %get-tuple-element.20, f32[1024]{0:T(1024)S(1)} %get-tuple-element.17, f32[1024]{0:T(1024)S(1)} %get-tuple-element.21, ...), channel_id=1, replica_groups=mesh['dp'=8,'tensor'=4] {'dp','tensor'}, use_global_device_ids=true, to_apply=%region_18.19 | all-reduce | flops 5120 | bytes 40960 | tf_op jit(solution)/shard_map/psum | solution.py:259
  502.5 27.6 %reduce-scatter.13.cloned.1.call-done = f32[256,128]{1,0:T(8,128)} async-done(((f32[256,1024]{1,0:T(8,128)}), f32[256,128]{1,0:T(8,128)}) %reduce-scatter.13.cloned.1.call-update) | async-done | bytes 131088 | tf_op jit(solution)/shard_map/reduce_scatter | solution.py:194
  530.1 77.3 %reduce-scatter.11.cloned.1.call-done = f32[128,768]{1,0:T(8,128)} async-done(((f32[1024,768]{1,0:T(8,128)}), f32[128,768]{1,0:T(8,128)}) %reduce-scatter.11.cloned.1.call-update) | async-done | bytes 393232 | tf_op jit(solution)/shard_map/reduce_scatter | solution.py:255
  607.4 91.6 %reduce-scatter.15.cloned.1.call-done = f32[128,1024]{1,0:T(8,128)} async-done(((f32[1024,1024]{1,0:T(8,128)}), f32[128,1024]{1,0:T(8,128)}) %reduce-scatter.15.cloned.1.call-update) | async-done | bytes 524304 | tf_op jit(solution)/shard_map/reduce_scatter | solution.py:195
  699.0 92.5 %reduce-scatter.17.cloned.1.call-done = f32[1024,128]{1,0:T(8,128)} async-done(((f32[1024,1024]{1,0:T(8,128)}), f32[1024,128]{1,0:T(8,128)}) %reduce-scatter.17.cloned.1.call-update) | async-done | bytes 524304 | tf_op jit(solution)/shard_map/reduce_scatter | solution.py:196
  (149 shorter events, 20.5 us)
Async XLA Ops:
  7.2 7.8 copy-start.20
  7.2 7.8 copy-start.17
  7.2 40.2 %all-gather.17.cloned.1.call-start = ((), (), s32[]{:S(2)}) async-start(), calls=%async_computation.12 | async-start | bytes 1310720 | tf_op jit(solution)/shard_map/all_gather | solution.py:178
  7.9 41.9 %all-gather.7.cloned.1.call-start = ((), (), s32[]{:S(2)}) async-start(), calls=%async_computation.6 | async-start | bytes 1310720 | tf_op jit(solution)/shard_map/all_gather | solution.py:99
  12.3 82.0 %all-gather.9.cloned.1.call-start = ((), (), s32[]{:S(2)}) async-start(), calls=%async_computation.7 | async-start | bytes 1769472 | tf_op jit(solution)/shard_map/all_gather | solution.py:108
  13.0 175.3 %all-gather.11.cloned.1.call-start = ((), (), s32[]{:S(2)}) async-start(), calls=%async_computation.8 | async-start | bytes 1310720 | tf_op jit(solution)/shard_map/all_gather | solution.py:102
  13.6 174.8 %all-gather.13.cloned.1.call-start = ((), (), s32[]{:S(2)}) async-start(), calls=%async_computation.9 | async-start | bytes 2359296 | tf_op jit(solution)/shard_map/all_gather | solution.py:110
  14.2 80.1 %copy-start.26 = (f32[768]{0:T(1024)S(1)}, f32[768]{0:T(1024)}, u32[]{:S(2)}) copy-start(f32[768]{0:T(1024)} %param.22) | copy-start | bytes 9220
  14.2 249.6 %all-gather.15.cloned.1.call-start = ((), (), s32[]{:S(2)}) async-start(), calls=%async_computation.10 | async-start | bytes 2359296 | tf_op jit(solution)/shard_map/all_gather | solution.py:111
  14.8 412.1 %reduce-scatter.9.cloned.1.call-start = ((), (), s32[]{:S(2)}) async-start(), calls=%async_computation.13 | async-start | bytes 5242880 | tf_op jit(solution)/shard_map/reduce_scatter | solution.py:239
  44.5 49.8 %copy-start.2 = (bf16[256,1024]{1,0:T(8,128)(2,1)}, bf16[256,1024]{1,0:T(8,128)(2,1)S(1)}, u32[]{:S(2)}) copy-start(bf16[256,1024]{1,0:T(8,128)(2,1)S(1)} %all_gather.27) | copy-start | bytes 1572868
  97.9 12.6 %collective-permute-start = (bf16[2,512,256]{1,2,0:T(8,128)(2,1)S(1)}, bf16[2,512,256]{1,2,0:T(8,128)(2,1)S(1)}, u32[]{:S(2)}, u32[]{:S(2)}) collective-permute-start(bf16[2,512,256]{1,2,0:T(8,128)(2,1)S(1)} %pad_maximum_fusion.6), channel_id=1, source_target_pairs={{0,4},{4,8},{8,12},{12,16},{16,20},{20,24},{24,28},{1,5},{5,9},{9,... | collective-permute-start | bytes 1572872 | tf_op jit(solution)/shard_map/ppermute | solution.py:18
  100.4 15.6 %collective-permute-start.1 = (bf16[2,512,256]{1,2,0:T(8,128)(2,1)S(1)}, bf16[2,512,256]{1,2,0:T(8,128)(2,1)S(1)}, u32[]{:S(2)}, u32[]{:S(2)}) collective-permute-start(bf16[2,512,256]{1,2,0:T(8,128)(2,1)S(1)} %pad_maximum_fusion.6), channel_id=1, source_target_pairs={{0,8},{4,12},{8,16},{12,20},{16,24},{20,28},{1,9},{5,13},{9,17},{1... | collective-permute-start | bytes 1572872 | tf_op jit(solution)/shard_map/ppermute | solution.py:18
  103.8 28.7 %collective-permute-start.2 = (bf16[2,512,256]{1,2,0:T(8,128)(2,1)S(1)}, bf16[2,512,256]{1,2,0:T(8,128)(2,1)S(1)}, u32[]{:S(2)}, u32[]{:S(2)}) collective-permute-start(bf16[2,512,256]{1,2,0:T(8,128)(2,1)S(1)} %pad_maximum_fusion.6), channel_id=1, source_target_pairs={{0,12},{4,16},{8,20},{12,24},{16,28},{1,13},{5,17},{9,21},{13,25},... | collective-permute-start | bytes 1572872 | tf_op jit(solution)/shard_map/ppermute | solution.py:18
  107.4 36.9 %collective-permute-start.3 = (bf16[2,512,256]{1,2,0:T(8,128)(2,1)S(1)}, bf16[2,512,256]{1,2,0:T(8,128)(2,1)S(1)}, u32[]{:S(2)}, u32[]{:S(2)}) collective-permute-start(bf16[2,512,256]{1,2,0:T(8,128)(2,1)S(1)} %pad_maximum_fusion.6), channel_id=1, source_target_pairs={{0,16},{4,20},{8,24},{12,28},{1,17},{5,21},{9,25},{13,29},{2,18},{... | collective-permute-start | bytes 1572872 | tf_op jit(solution)/shard_map/ppermute | solution.py:18
  108.8 1.8 copy-start.7
  110.6 5.5 copy-start.6
  116.1 39.4 %copy-start.15 = (bf16[1,512,256]{1,2,0:T(8,128)(2,1)}, bf16[1,512,256]{1,2,0:T(8,128)(2,1)S(1)}, u32[]{:S(2)}) copy-start(bf16[1,512,256]{1,2,0:T(8,128)(2,1)S(1)} %get-tuple-element.39) | copy-start | bytes 786436
  116.1 16.4 %copy-start.5 = (pred[512,512]{0,1:T(8,128)(4,1)S(1)}, pred[512,512]{0,1:T(8,128)(4,1)}, u32[]{:S(2)}) copy-start(pred[512,512]{0,1:T(8,128)(4,1)} %get-tuple-element.66) | copy-start | bytes 786436
  132.5 1.0 copy-start.10
  132.5 11.9 %copy-start.4 = (pred[512,512]{0,1:T(8,128)(4,1)S(1)}, pred[512,512]{0,1:T(8,128)(4,1)}, u32[]{:S(2)}) copy-start(pred[512,512]{0,1:T(8,128)(4,1)} %get-tuple-element.67) | copy-start | bytes 786436
  144.4 0.9 copy-start.12
  154.2 1.3 copy-start.28
  162.4 1.6 copy-start.16
  172.8 96.5 %collective-permute-start.4 = (f32[2,512,256]{1,2,0:T(8,128)}, f32[2,512,256]{1,2,0:T(8,128)}, u32[]{:S(2)}, u32[]{:S(2)}) collective-permute-start(f32[2,512,256]{1,2,0:T(8,128)} %pad_maximum_fusion.2), channel_id=1, source_target_pairs={{4,0},{8,4},{12,8},{16,12},{20,16},{24,20},{28,24},{5,1},{9,5},{13... | collective-permute-start | bytes 3145736 | tf_op jit(solution)/shard_map/ppermute | solution.py:18
  175.9 93.5 %collective-permute-start.5 = (f32[2,512,256]{1,2,0:T(8,128)}, f32[2,512,256]{1,2,0:T(8,128)}, u32[]{:S(2)}, u32[]{:S(2)}) collective-permute-start(f32[2,512,256]{1,2,0:T(8,128)} %pad_maximum_fusion.3), channel_id=1, source_target_pairs={{8,0},{12,4},{16,8},{20,12},{24,16},{28,20},{9,1},{13,5},{17,9},{2... | collective-permute-start | bytes 3145736 | tf_op jit(solution)/shard_map/ppermute | solution.py:18
  179.0 111.7 %collective-permute-start.6 = (f32[2,512,256]{1,2,0:T(8,128)}, f32[2,512,256]{1,2,0:T(8,128)}, u32[]{:S(2)}, u32[]{:S(2)}) collective-permute-start(f32[2,512,256]{1,2,0:T(8,128)} %pad_maximum_fusion.4), channel_id=1, source_target_pairs={{12,0},{16,4},{20,8},{24,12},{28,16},{13,1},{17,5},{21,9},{25,13},... | collective-permute-start | bytes 3145736 | tf_op jit(solution)/shard_map/ppermute | solution.py:18
  181.0 2.9 copy-start.11
  182.1 195.0 %collective-permute-start.7 = (f32[2,512,256]{1,2,0:T(8,128)}, f32[2,512,256]{1,2,0:T(8,128)}, u32[]{:S(2)}, u32[]{:S(2)}) collective-permute-start(f32[2,512,256]{1,2,0:T(8,128)} %pad_maximum_fusion.5), channel_id=1, source_target_pairs={{16,0},{20,4},{24,8},{28,12},{17,1},{21,5},{25,9},{29,13},{18,2},{... | collective-permute-start | bytes 3145736 | tf_op jit(solution)/shard_map/ppermute | solution.py:18
  183.9 1.0 copy-start.13
  187.1 1.3 copy-start.27
  188.3 75.5 %copy-start.1 = (bf16[512,1024]{1,0:T(8,128)(2,1)S(1)}, bf16[512,1024]{1,0:T(8,128)(2,1)}, u32[]{:S(2)}) copy-start(bf16[512,1024]{1,0:T(8,128)(2,1)} %all-gather.17.cloned.1.call-done) | copy-start | bytes 3145732
  263.8 4.2 copy-start.24
  268.0 1.3 copy-start.14
  380.2 1.4 copy-start.25
  385.0 75.7 %reduce-scatter.7.cloned.1.call-start = ((), (), s32[]{:S(2)}) async-start(), calls=%async_computation.11 | async-start | bytes 2621440 | tf_op jit(solution)/shard_map/reduce_scatter | solution.py:170
  385.0 3.3 copy-start.3
  385.0 3.3 copy-start.8
  390.1 140.0 %reduce-scatter.13.cloned.1.call-start = ((), (), s32[]{:S(2)}) async-start(), calls=%async_computation.15 | async-start | bytes 1179648 | tf_op jit(solution)/shard_map/reduce_scatter | solution.py:194
  392.6 214.8 %reduce-scatter.11.cloned.1.call-start = ((), (), s32[]{:S(2)}) async-start(), calls=%async_computation.14 | async-start | bytes 3538944 | tf_op jit(solution)/shard_map/reduce_scatter | solution.py:255
  396.7 302.4 %reduce-scatter.15.cloned.1.call-start = ((), (), s32[]{:S(2)}) async-start(), calls=%async_computation.16 | async-start | bytes 4718592 | tf_op jit(solution)/shard_map/reduce_scatter | solution.py:195
  401.7 389.8 %reduce-scatter.17.cloned.1.call-start = ((), (), s32[]{:S(2)}) async-start(), calls=%async_computation.17 | async-start | bytes 4718592 | tf_op jit(solution)/shard_map/reduce_scatter | solution.py:196
  406.4 21.8 %copy-start = (bf16[128,1024]{1,0:T(8,128)(2,1)S(1)}, bf16[128,1024]{1,0:T(8,128)(2,1)}, u32[]{:S(2)}) copy-start(bf16[128,1024]{1,0:T(8,128)(2,1)} %param.15) | copy-start | bytes 786436
  406.4 21.8 %copy-start.18 = (f32[1024]{0:T(1024)S(1)}, f32[1024]{0:T(1024)}, u32[]{:S(2)}) copy-start(f32[1024]{0:T(1024)} %param.17) | copy-start | bytes 12292
  406.4 21.8 %copy-start.19 = (f32[1024]{0:T(1024)S(1)}, f32[1024]{0:T(1024)}, u32[]{:S(2)}) copy-start(f32[1024]{0:T(1024)} %param.19) | copy-start | bytes 12292
  406.4 54.2 %copy-start.9 = (bf16[128,1024]{1,0:T(8,128)(2,1)S(1)}, bf16[128,1024]{1,0:T(8,128)(2,1)}, u32[]{:S(2)}) copy-start(bf16[128,1024]{1,0:T(8,128)(2,1)} %param.29) | copy-start | bytes 786436
  406.4 54.2 %copy-start.21 = (f32[1024]{0:T(1024)S(1)}, f32[1024]{0:T(1024)}, u32[]{:S(2)}) copy-start(f32[1024]{0:T(1024)} %param.28) | copy-start | bytes 12292
  406.5 54.2 %copy-start.22 = (f32[1024]{0:T(1024)S(1)}, f32[1024]{0:T(1024)}, u32[]{:S(2)}) copy-start(f32[1024]{0:T(1024)} %param.24) | copy-start | bytes 12292
  502.5 289.6 %copy-start.23 = (f32[1024]{0:T(1024)}, f32[1024]{0:T(1024)S(1)}, u32[]{:S(2)}) copy-start(f32[1024]{0:T(1024)S(1)} %get-tuple-element.130) | copy-start | bytes 12292
Sparse Core Ops, SparseCore 0:
  9.6 19.4 all-gather.16
  31.2 16.6 all-gather.6
  50.1 44.2 all-gather.8
  96.3 15.0 all-gather.10
  113.4 72.5 all-gather.12
  187.8 75.9 all-gather.14
  385.1 41.7 reduce-scatter.8
  429.4 31.1 reduce-scatter.6
  464.6 65.4 reduce-scatter.12
  534.1 73.2 reduce-scatter.10
  611.6 87.3 reduce-scatter.14
  703.1 88.3 reduce-scatter.16
where the time goes:
time: 807 us; the launch traced here: 799 us
  waiting for transfers between devices  576 us (71%)
  blocking collectives  87.3 us (11%)
  matrix products  73.6 us (9%)
  other arithmetic  27.3 us (3%)
  starting transfers between devices  16.6 us (2%)
  between operations  15.3 us (2%)
    ppermute x8, waiting for transfers between devices, shifted_2(): return lax.ppermute(shard, axis, pairs)  139 us
    reduce_scatter x1, waiting for transfers between devices, shards(): lax.psum_scatter(rows_product(hidden, grad_rows), 'dp', scatter_dimension...  92.5 us
    reduce_scatter x1, waiting for transfers between devices, shards(): lax.psum_scatter(rows_product(second_in, dpreact_b), 'dp', scatter_dimens...  91.6 us
    reduce_scatter x1, waiting for transfers between devices, shards(): lax.psum_scatter(rows_product(first_in, dfused_b), 'dp', scatter_dimensio...  77.3 us
    all_gather x1, waiting for transfers between devices, shards(): lax.all_gather(w_down, 'dp', axis=1, tiled=True)  66.6 us
    all_gather x1, waiting for transfers between devices, shards(): lax.all_gather(w_qkv, 'dp', axis=0, tiled=True)  44.5 us
    psum x1, blocking collectives, shards(): lax.psum((jnp.sum(dfirst * normed, axis=0), jnp.sum(dfirst, axis=0), jnp....  39.8 us
    reduce_scatter x1, waiting for transfers between devices, shards(): lax.psum_scatter(jnp.dot(context_b, full_out, preferred_element_type=jnp....  30.9 us
  transfers between devices with their start and end apart: 20, of which 14 were waited for; matrix products, arithmetic and copies ran while one was open for 12% of the time, Pallas kernels for 0%

commit v1 on v0

--- a/solution.py
+++ b/solution.py
@@ -10,6 +10,11 @@
 REACH = 4
 EPS = 1e-05
 MASKED = -1e30
+
+
+def gather_over(x, mesh_axis, d):
+    sent = jnp.stack([x] * lax.axis_size(mesh_axis))
+    return jnp.concatenate(lax.all_to_all(sent, mesh_axis, 0, 0), axis=d)
 
 
 def shifted_2(shard, axis, by):
@@ -105,7 +110,7 @@
     )
     row_count = first_in.shape[0]
     weights = (
-        lax.all_gather(w_qkv, "dp", axis=0, tiled=True),
+        gather_over(w_qkv, "dp", 0),
         lax.all_gather(w_out, "dp", axis=1, tiled=True),
         lax.all_gather(w_up, "dp", axis=0, tiled=True),
         lax.all_gather(w_down, "dp", axis=1, tiled=True),

time: 807 us -> 811 us (level)
  waiting for transfers between devices: 576 us -> 542 us
  blocking collectives: 87.3 us -> 115 us
    ppermute x8, waiting for transfers between devices: 139 us -> 216 us  [shifted_2(): return lax.ppermute(shard, axis, pairs)]
    all_gather x1, waiting for transfers between devices: 66.6 us -> 0.55 us  [shards(): lax.all_gather(w_down, 'dp', axis=1, tiled=True)]
    all_gather x1, waiting for transfers between devices: 44.5 us -> 0.02 us  [shards(): lax.all_gather(w_qkv, 'dp', axis=0, tiled=True)]
    all_gather x1, blocking collectives: 29.6 us -> 57.1 us  [shards(): lax.all_gather(w_out, 'dp', axis=1, tiled=True)]
  transfers between devices with their start and end apart: 20 -> 21, of which waited for: 14 -> 15; matrix products, arithmetic and copies ran while one was open for 12% -> 13% of each run, Pallas kernels for 0% -> 0%
where the time goes in v1:
time: 811 us; the launch traced here: 803 us
  waiting for transfers between devices  542 us (67%)
  blocking collectives  115 us (14%)
  matrix products  78 us (10%)
  other arithmetic  25.5 us (3%)
  starting transfers between devices  21.9 us (3%)
  between operations  15.2 us (2%)
    ppermute x8, waiting for transfers between devices, shifted_2(): return lax.ppermute(shard, axis, pairs)  216 us
    reduce_scatter x1, waiting for transfers between devices, shards(): lax.psum_scatter(rows_product(hidden, grad_rows), 'dp', scatter_dimension...  92.5 us
    reduce_scatter x1, waiting for transfers between devices, shards(): lax.psum_scatter(rows_product(second_in, dpreact_b), 'dp', scatter_dimens...  91.6 us
    reduce_scatter x1, waiting for transfers between devices, shards(): lax.psum_scatter(rows_product(first_in, dfused_b), 'dp', scatter_dimensio...  77.5 us
    all_gather x1, blocking collectives, shards(): lax.all_gather(w_out, 'dp', axis=1, tiled=True)  57.1 us
    psum x1, blocking collectives, shards(): lax.psum((jnp.sum(dfirst * normed, axis=0), jnp.sum(dfirst, axis=0), jnp....  39.8 us
    reduce_scatter x1, waiting for transfers between devices, shards(): lax.psum_scatter(jnp.dot(context_b, full_out, preferred_element_type=jnp....  30.9 us
    reduce_scatter x1, waiting for transfers between devices, shards(): lax.psum_scatter(rows_product(context_b, grad_rows), 'dp', scatter_dimens...  27.7 us
  transfers between devices with their start and end apart: 21, of which 15 were waited for; matrix products, arithmetic and copies ran while one was open for 13% of the time, Pallas kernels for 0%

profile of v1, /device:TPU:0, one launch (start us, length us, event | category | flops | bytes accessed | tf_op | source)
XLA Modules:
  0.0 802.5 jit_solution(16299015918187358122)
XLA Ops:
  9.0 1.2 fusion.63
  10.2 2.0 fusion.55
  14.2 1.3 stack.47
  15.5 7.4 all-to-all-start
  23.9 57.1 %all_gather.25 = bf16[256,1024]{1,0:T(8,128)(2,1)S(1)} all-gather(bf16[256,128]{1,0:T(8,128)(2,1)S(1)} %copy-done.16), channel_id=1, replica_groups=mesh['dp'=8,'tensor'=4] {'dp'}, dimensions={1}, use_global_device_ids=true | all-gather | bytes 589824 | tf_op jit(solution)/shard_map/all_gather | solution.py:114
  81.0 1.9 fusion.39
  82.9 2.4 convolution_convert_fusion
  85.3 3.4 convolution_add_fusion.1
  88.7 1.9 copy.87
  91.0 1.3 collective-permute-start
  92.3 3.0 collective-permute-start.1
  95.3 2.4 collective-permute-start.2
  97.7 1.9 collective-permute-start.3
  100.5 6.4 collective-permute-done
  107.9 10.6 %collective-permute-done.1 = bf16[2,512,256]{1,2,0:T(8,128)(2,1)S(1)} collective-permute-done((bf16[2,512,256]{1,2,0:T(8,128)(2,1)S(1)}, bf16[2,512,256]{1,2,0:T(8,128)(2,1)S(1)}, u32[]{:S(2)}, u32[]{:S(2)}) %collective-permute-start.1) | collective-permute-done | bytes 524320 | tf_op jit(solution)/shard_map/ppermute | solution.py:23
  119.4 15.8 %collective-permute-done.2 = bf16[2,512,256]{1,2,0:T(8,128)(2,1)S(1)} collective-permute-done((bf16[2,512,256]{1,2,0:T(8,128)(2,1)S(1)}, bf16[2,512,256]{1,2,0:T(8,128)(2,1)S(1)}, u32[]{:S(2)}, u32[]{:S(2)}) %collective-permute-start.2) | collective-permute-done | bytes 524320 | tf_op jit(solution)/shard_map/ppermute | solution.py:23
  136.2 4.6 collective-permute-done.3
  141.8 5.1 exponential_reduce_fusion.3
  146.9 1.2 fusion.73
  148.2 1.3 fusion.108
  149.4 1.3 fusion.104
  150.7 1.3 convolution_add_fusion.5
  152.0 2.0 multiply_reduce_fusion
  154.0 1.6 multiply_convert_fusion.4
  155.6 1.6 multiply_convert_fusion.3
  157.2 1.6 multiply_convert_fusion.1
  158.9 1.6 multiply_convert_fusion
  160.5 1.8 multiply_convert_fusion.2
  163.5 2.0 fusion.99
  165.6 1.2 fusion.96
  166.8 1.3 fusion.93
  169.3 1.3 fusion.106
  171.8 1.3 fusion.102
  174.4 1.3 collective-permute-start.4
  177.5 1.3 collective-permute-start.5
  179.9 1.3 collective-permute-start.6
  182.3 1.4 collective-permute-start.7
  184.3 8.8 %fusion.12 = (bf16[512,1024]{1,0:T(8,128)(2,1)}, f32[512,1024]{1,0:T(8,128)}) fusion(f32[1024]{0:T(1024)S(1)} %copy-done.25, bf16[512,1024]{1,0:T(8,128)(2,1)} %all-gather.9.cloned.1.call-done, bf16[1024,1024]{1,0:T(8,128)(2,1)} %all-gather.11.cloned.1.call-done), kind=kOutput, calls=%fused_computation.35 | convolution fusion | flops 1108344832 | bytes 6295552 | tf_op jit(solution)/shard_map/dot_general | solution.py:173
  193.7 4.2 fusion.129
  197.9 2.6 convolution_bitcast_fusion
  200.5 8.9 %collective-permute-done.4 = f32[2,512,256]{1,2,0:T(8,128)} collective-permute-done((f32[2,512,256]{1,2,0:T(8,128)S(1)}, f32[2,512,256]{1,2,0:T(8,128)}, u32[]{:S(2)}, u32[]{:S(2)}) %collective-permute-start.4) | collective-permute-done | bytes 1048608 | tf_op jit(solution)/shard_map/ppermute | solution.py:23
  209.4 47.0 %collective-permute-done.5 = f32[2,512,256]{1,2,0:T(8,128)} collective-permute-done((f32[2,512,256]{1,2,0:T(8,128)}, f32[2,512,256]{1,2,0:T(8,128)}, u32[]{:S(2)}, u32[]{:S(2)}) %collective-permute-start.5) | collective-permute-done | bytes 1048608 | tf_op jit(solution)/shard_map/ppermute | solution.py:23
  256.4 33.0 %collective-permute-done.6 = f32[2,512,256]{1,2,0:T(8,128)} collective-permute-done((f32[2,512,256]{1,2,0:T(8,128)}, f32[2,512,256]{1,2,0:T(8,128)}, u32[]{:S(2)}, u32[]{:S(2)}) %collective-permute-start.6) | collective-permute-done | bytes 1048608 | tf_op jit(solution)/shard_map/ppermute | solution.py:23
  289.4 89.9 %collective-permute-done.7 = f32[2,512,256]{1,2,0:T(8,128)} collective-permute-done((f32[2,512,256]{1,2,0:T(8,128)}, f32[2,512,256]{1,2,0:T(8,128)}, u32[]{:S(2)}, u32[]{:S(2)}) %collective-permute-start.7) | collective-permute-done | bytes 1048608 | tf_op jit(solution)/shard_map/ppermute | solution.py:23
  379.3 2.8 fusion.35
  383.3 2.6 convolution_bitcast_fusion.1
  385.9 2.3 pad_maximum_fusion
  388.3 3.2 fusion.133
  391.6 1.8 convolution_add_fusion
  393.4 2.4 fusion.137
  395.9 4.0 fusion.136
  400.0 4.9 fusion.69
  405.2 4.5 fusion.138
  410.0 17.9 %all-reduce.1 = (f32[768]{0:T(1024)}, f32[1024]{0:T(1024)}) all-reduce(f32[768]{0:T(1024)S(1)} %reduce_sum.170, f32[1024]{0:T(1024)S(1)} %get-tuple-element.85), channel_id=1, replica_groups=mesh['dp'=8,'tensor'=4] {'dp'}, use_global_device_ids=true, to_apply=%region_27.28 | all-reduce | flops 1792 | bytes 14336 | tf_op jit(solution)/shard_map/psum | solution.py:263
  428.0 2.0 reduce-scatter.9.cloned.1.call-done
  430.0 1.3 slice_reduce_fusion
  431.3 1.5 fusion.120
  432.8 30.9 %reduce-scatter.7.cloned.1.call-done = f32[128,1024]{1,0:T(8,128)} async-done(((f32[512,1024]{1,0:T(8,128)}), f32[128,1024]{1,0:T(8,128)}) %reduce-scatter.7.cloned.1.call-update) | async-done | bytes 524304 | tf_op jit(solution)/shard_map/reduce_scatter | solution.py:175
  463.7 2.1 convert_reduce_fusion.1
  465.8 39.8 %all-reduce = (f32[1024]{0:T(1024)}, f32[1024]{0:T(1024)}, f32[1024]{0:T(1024)}, f32[1024]{0:T(1024)}, f32[1024]{0:T(1024)S(1)}) all-reduce(f32[1024]{0:T(1024)S(1)} %get-tuple-element.20, f32[1024]{0:T(1024)S(1)} %get-tuple-element.17, f32[1024]{0:T(1024)S(1)} %get-tuple-element.21, ...), channel_id=1, replica_groups=mesh['dp'=8,'tensor'=4] {'dp','tensor'}, use_global_device_ids=true, to_apply=%region_18.19 | all-reduce | flops 5120 | bytes 40960 | tf_op jit(solution)/shard_map/psum | solution.py:264
  505.6 27.7 %reduce-scatter.13.cloned.1.call-done = f32[256,128]{1,0:T(8,128)} async-done(((f32[256,1024]{1,0:T(8,128)}), f32[256,128]{1,0:T(8,128)}) %reduce-scatter.13.cloned.1.call-update) | async-done | bytes 131088 | tf_op jit(solution)/shard_map/reduce_scatter | solution.py:199
  533.3 77.5 %reduce-scatter.11.cloned.1.call-done = f32[128,768]{1,0:T(8,128)} async-done(((f32[1024,768]{1,0:T(8,128)}), f32[128,768]{1,0:T(8,128)}) %reduce-scatter.11.cloned.1.call-update) | async-done | bytes 393232 | tf_op jit(solution)/shard_map/reduce_scatter | solution.py:260
  610.8 91.6 %reduce-scatter.15.cloned.1.call-done = f32[128,1024]{1,0:T(8,128)} async-done(((f32[1024,1024]{1,0:T(8,128)}), f32[128,1024]{1,0:T(8,128)}) %reduce-scatter.15.cloned.1.call-update) | async-done | bytes 524304 | tf_op jit(solution)/shard_map/reduce_scatter | solution.py:200
  702.4 92.5 %reduce-scatter.17.cloned.1.call-done = f32[1024,128]{1,0:T(8,128)} async-done(((f32[1024,1024]{1,0:T(8,128)}), f32[1024,128]{1,0:T(8,128)}) %reduce-scatter.17.cloned.1.call-update) | async-done | bytes 524304 | tf_op jit(solution)/shard_map/reduce_scatter | solution.py:201
  (148 shorter events, 22.3 us)
Async XLA Ops:
  7.2 7.0 copy-start.10
  7.2 75.7 %all-gather.15.cloned.1.call-start = ((), (), s32[]{:S(2)}) async-start(), calls=%async_computation.12 | async-start | bytes 1310720 | tf_op jit(solution)/shard_map/all_gather | solution.py:183
  7.9 77.4 %all-gather.7.cloned.1.call-start = ((), (), s32[]{:S(2)}) async-start(), calls=%async_computation.7 | async-start | bytes 1310720 | tf_op jit(solution)/shard_map/all_gather | solution.py:104
  12.3 172.0 %all-gather.9.cloned.1.call-start = ((), (), s32[]{:S(2)}) async-start(), calls=%async_computation.8 | async-start | bytes 1310720 | tf_op jit(solution)/shard_map/all_gather | solution.py:107
  13.0 171.3 %all-gather.11.cloned.1.call-start = ((), (), s32[]{:S(2)}) async-start(), calls=%async_computation.9 | async-start | bytes 2359296 | tf_op jit(solution)/shard_map/all_gather | solution.py:115
  13.6 180.1 %all-gather.13.cloned.1.call-start = ((), (), s32[]{:S(2)}) async-start(), calls=%async_computation.10 | async-start | bytes 2359296 | tf_op jit(solution)/shard_map/all_gather | solution.py:116
  15.5 8.1 %copy-start.19 = (s32[512]{0:T(512)S(1)}, s32[512]{0:T(512)}, u32[]{:S(2)}) copy-start(s32[512]{0:T(512)} %param.16) | copy-start | bytes 6148
  15.5 8.4 %copy-start.16 = (bf16[256,128]{1,0:T(8,128)(2,1)S(1)}, bf16[256,128]{1,0:T(8,128)(2,1)}, u32[]{:S(2)}) copy-start(bf16[256,128]{1,0:T(8,128)(2,1)} %param.23) | copy-start | bytes 196612
  15.5 69.9 %all-to-all-start = ((bf16[8,128,768]{2,1,0:T(8,128)(2,1)}), bf16[8,128,768]{2,1,0:T(8,128)(2,1)S(1)}, u32[]{:S(2)}, u32[]{:S(2)}) async-start(bf16[8,128,768]{2,1,0:T(8,128)(2,1)} %stack.47), calls=%async_computation | async-start | bytes 3145728 | tf_op jit(solution)/shard_map/all_to_all | solution.py:17
  22.9 62.4 %copy-start.24 = (f32[768]{0:T(1024)S(1)}, f32[768]{0:T(1024)}, u32[]{:S(2)}) copy-start(f32[768]{0:T(1024)} %param.22) | copy-start | bytes 9220
  22.9 360.4 %all-gather.17.cloned.1.call-start = ((), (), s32[]{:S(2)}) async-start(), calls=%async_computation.13 | async-start | bytes 1769472 | tf_op jit(solution)/shard_map/all_gather | solution.py:185
  23.5 406.5 %reduce-scatter.9.cloned.1.call-start = ((), (), s32[]{:S(2)}) async-start(), calls=%async_computation.14 | async-start | bytes 5242880 | tf_op jit(solution)/shard_map/reduce_scatter | solution.py:244
  23.8 75.7 %copy-start.12 = (f32[512,16]{0,1:T(8,128)}, f32[512,16]{0,1:T(8,128)S(1)}, u32[]{:S(2)}) copy-start(f32[512,16]{0,1:T(8,128)S(1)} %get-tuple-element.99) | copy-start | bytes 98308
  23.8 75.7 %copy-start.14 = (f32[512,16]{0,1:T(8,128)}, f32[512,16]{0,1:T(8,128)S(1)}, u32[]{:S(2)}) copy-start(f32[512,16]{0,1:T(8,128)S(1)} %get-tuple-element.100) | copy-start | bytes 98308
  80.9 4.4 copy-start.2
  91.0 15.9 %collective-permute-start = (bf16[2,512,256]{1,2,0:T(8,128)(2,1)S(1)}, bf16[2,512,256]{1,2,0:T(8,128)(2,1)S(1)}, u32[]{:S(2)}, u32[]{:S(2)}) collective-permute-start(bf16[2,512,256]{1,2,0:T(8,128)(2,1)S(1)} %pad_maximum_fusion.6), channel_id=1, source_target_pairs={{0,4},{4,8},{8,12},{12,16},{16,20},{20,24},{24,28},{1,5},{5,9},{9,... | collective-permute-start | bytes 1572872 | tf_op jit(solution)/shard_map/ppermute | solution.py:23
  92.3 26.2 %collective-permute-start.1 = (bf16[2,512,256]{1,2,0:T(8,128)(2,1)S(1)}, bf16[2,512,256]{1,2,0:T(8,128)(2,1)S(1)}, u32[]{:S(2)}, u32[]{:S(2)}) collective-permute-start(bf16[2,512,256]{1,2,0:T(8,128)(2,1)S(1)} %pad_maximum_fusion.6), channel_id=1, source_target_pairs={{0,8},{4,12},{8,16},{12,20},{16,24},{20,28},{1,9},{5,13},{9,17},{1... | collective-permute-start | bytes 1572872 | tf_op jit(solution)/shard_map/ppermute | solution.py:23
  95.3 39.9 %collective-permute-start.2 = (bf16[2,512,256]{1,2,0:T(8,128)(2,1)S(1)}, bf16[2,512,256]{1,2,0:T(8,128)(2,1)S(1)}, u32[]{:S(2)}, u32[]{:S(2)}) collective-permute-start(bf16[2,512,256]{1,2,0:T(8,128)(2,1)S(1)} %pad_maximum_fusion.6), channel_id=1, source_target_pairs={{0,12},{4,16},{8,20},{12,24},{16,28},{1,13},{5,17},{9,21},{13,25},... | collective-permute-start | bytes 1572872 | tf_op jit(solution)/shard_map/ppermute | solution.py:23
  97.7 43.2 %collective-permute-start.3 = (bf16[2,512,256]{1,2,0:T(8,128)(2,1)S(1)}, bf16[2,512,256]{1,2,0:T(8,128)(2,1)S(1)}, u32[]{:S(2)}, u32[]{:S(2)}) collective-permute-start(bf16[2,512,256]{1,2,0:T(8,128)(2,1)S(1)} %pad_maximum_fusion.6), channel_id=1, source_target_pairs={{0,16},{4,20},{8,24},{12,28},{1,17},{5,21},{9,25},{13,29},{2,18},{... | collective-permute-start | bytes 1572872 | tf_op jit(solution)/shard_map/ppermute | solution.py:23
  118.5 0.9 copy-start.6
  150.7 1.3 copy-start.26
  174.4 35.0 %collective-permute-start.4 = (f32[2,512,256]{1,2,0:T(8,128)S(1)}, f32[2,512,256]{1,2,0:T(8,128)}, u32[]{:S(2)}, u32[]{:S(2)}) collective-permute-start(f32[2,512,256]{1,2,0:T(8,128)S(1)} %pad_maximum_fusion.2), channel_id=1, source_target_pairs={{4,0},{8,4},{12,8},{16,12},{20,16},{24,20},{28,24},{5,1},{9,5},{13... | collective-permute-start | bytes 3145736 | tf_op jit(solution)/shard_map/ppermute | solution.py:23
  177.5 78.9 %collective-permute-start.5 = (f32[2,512,256]{1,2,0:T(8,128)}, f32[2,512,256]{1,2,0:T(8,128)}, u32[]{:S(2)}, u32[]{:S(2)}) collective-permute-start(f32[2,512,256]{1,2,0:T(8,128)} %pad_maximum_fusion.3), channel_id=1, source_target_pairs={{8,0},{12,4},{16,8},{20,12},{24,16},{28,20},{9,1},{13,5},{17,9},{2... | collective-permute-start | bytes 3145736 | tf_op jit(solution)/shard_map/ppermute | solution.py:23
  178.8 4.9 copy-start.7
  179.9 109.5 %collective-permute-start.6 = (f32[2,512,256]{1,2,0:T(8,128)}, f32[2,512,256]{1,2,0:T(8,128)}, u32[]{:S(2)}, u32[]{:S(2)}) collective-permute-start(f32[2,512,256]{1,2,0:T(8,128)} %pad_maximum_fusion.4), channel_id=1, source_target_pairs={{12,0},{16,4},{20,8},{24,12},{28,16},{13,1},{17,5},{21,9},{25,13},... | collective-permute-start | bytes 3145736 | tf_op jit(solution)/shard_map/ppermute | solution.py:23
  182.3 2.0 copy-start.25
  182.3 197.0 %collective-permute-start.7 = (f32[2,512,256]{1,2,0:T(8,128)}, f32[2,512,256]{1,2,0:T(8,128)}, u32[]{:S(2)}, u32[]{:S(2)}) collective-permute-start(f32[2,512,256]{1,2,0:T(8,128)} %pad_maximum_fusion.5), channel_id=1, source_target_pairs={{16,0},{20,4},{24,8},{28,12},{17,1},{21,5},{25,9},{29,13},{18,2},{... | collective-permute-start | bytes 3145736 | tf_op jit(solution)/shard_map/ppermute | solution.py:23
  184.2 9.5 %copy-start.1 = (bf16[512,1024]{1,0:T(8,128)(2,1)S(1)}, bf16[512,1024]{1,0:T(8,128)(2,1)}, u32[]{:S(2)}) copy-start(bf16[512,1024]{1,0:T(8,128)(2,1)} %all-gather.15.cloned.1.call-done) | copy-start | bytes 3145732
  193.7 4.2 copy-start.23
  197.9 2.7 copy-start.9
  197.9 181.4 %copy-start.11 = (f32[4,64,512]{2,1,0:T(8,128)S(1)}, f32[4,64,512]{2,1,0:T(8,128)}, u32[]{:S(2)}) copy-start(f32[4,64,512]{2,1,0:T(8,128)} %fusion.99) | copy-start | bytes 1572868
  382.1 0.8 copy-start.15
  382.1 0.8 copy-start.13
  383.3 2.6 copy-start.4
  388.2 75.5 %reduce-scatter.7.cloned.1.call-start = ((), (), s32[]{:S(2)}) async-start(), calls=%async_computation.11 | async-start | bytes 2621440 | tf_op jit(solution)/shard_map/reduce_scatter | solution.py:175
  388.3 3.3 copy-start.3
  388.3 3.3 copy-start.5
  393.4 140.0 %reduce-scatter.13.cloned.1.call-start = ((), (), s32[]{:S(2)}) async-start(), calls=%async_computation.16 | async-start | bytes 1179648 | tf_op jit(solution)/shard_map/reduce_scatter | solution.py:199
  395.9 214.9 %reduce-scatter.11.cloned.1.call-start = ((), (), s32[]{:S(2)}) async-start(), calls=%async_computation.15 | async-start | bytes 3538944 | tf_op jit(solution)/shard_map/reduce_scatter | solution.py:260
  399.9 302.5 %reduce-scatter.15.cloned.1.call-start = ((), (), s32[]{:S(2)}) async-start(), calls=%async_computation.17 | async-start | bytes 4718592 | tf_op jit(solution)/shard_map/reduce_scatter | solution.py:200
  405.0 389.9 %reduce-scatter.17.cloned.1.call-start = ((), (), s32[]{:S(2)}) async-start(), calls=%async_computation.18 | async-start | bytes 4718592 | tf_op jit(solution)/shard_map/reduce_scatter | solution.py:201
  409.7 21.6 %copy-start = (bf16[128,1024]{1,0:T(8,128)(2,1)S(1)}, bf16[128,1024]{1,0:T(8,128)(2,1)}, u32[]{:S(2)}) copy-start(bf16[128,1024]{1,0:T(8,128)(2,1)} %param.15) | copy-start | bytes 786436
  409.7 21.6 %copy-start.17 = (f32[1024]{0:T(1024)S(1)}, f32[1024]{0:T(1024)}, u32[]{:S(2)}) copy-start(f32[1024]{0:T(1024)} %param.17) | copy-start | bytes 12292
  409.7 21.6 %copy-start.18 = (f32[1024]{0:T(1024)S(1)}, f32[1024]{0:T(1024)}, u32[]{:S(2)}) copy-start(f32[1024]{0:T(1024)} %param.19) | copy-start | bytes 12292
  409.7 54.0 %copy-start.8 = (bf16[128,1024]{1,0:T(8,128)(2,1)S(1)}, bf16[128,1024]{1,0:T(8,128)(2,1)}, u32[]{:S(2)}) copy-start(bf16[128,1024]{1,0:T(8,128)(2,1)} %param.29) | copy-start | bytes 786436
  409.7 54.0 %copy-start.20 = (f32[1024]{0:T(1024)S(1)}, f32[1024]{0:T(1024)}, u32[]{:S(2)}) copy-start(f32[1024]{0:T(1024)} %param.28) | copy-start | bytes 12292
  409.7 54.0 %copy-start.21 = (f32[1024]{0:T(1024)S(1)}, f32[1024]{0:T(1024)}, u32[]{:S(2)}) copy-start(f32[1024]{0:T(1024)} %param.24) | copy-start | bytes 12292
  505.6 289.9 %copy-start.22 = (f32[1024]{0:T(1024)}, f32[1024]{0:T(1024)S(1)}, u32[]{:S(2)}) copy-start(f32[1024]{0:T(1024)S(1)} %get-tuple-element.130) | copy-start | bytes 12292
Sparse Core Ops, SparseCore 0:
  9.6 19.4 all-gather.14
  31.1 16.6 all-gather.6
  50.0 16.6 all-gather.8
  68.7 60.8 all-gather.10
  131.5 62.1 all-gather.12
  195.7 57.0 all-gather.16
  388.4 41.5 reduce-scatter.8
  432.5 31.1 reduce-scatter.6
  467.7 65.6 reduce-scatter.12
  537.3 73.4 reduce-scatter.10
  615.0 87.3 reduce-scatter.14
  706.5 88.3 reduce-scatter.16
